TPU v7x, 256 devices: a whole 4x4x8 slice. The times are simulated.
256 devices in a mesh: rows: 64 (over x_hi, y, z), grp: 4 (over x_lo, core).
Axes of the slice: x: 4 (x_hi: 2, x_lo: 2; x = x_hi * 2 + x_lo), y: 4, z: 8, core: 2. Of those that a mesh axis runs over, the one named last changes fastest.
Arguments:
- table: float32 [524288, 256], P(('rows', 'grp')), may hold values from -1.5 to 1.5
- hot_slot: int32 [4096], P(('rows', 'grp')), may hold values from 0 to 2047, as said below
- cold_row: int32 [256, 256, 8], P(('rows', 'grp')), may hold values from 0 to 2047, as said below
- cold_bag: int32 [256, 256, 8], P(('rows', 'grp')), may hold values from 0 to 511
- hot_pick: int32 [65536, 8], P(('rows', 'grp')), may hold values from 0 to 4095
- dense: float32 [65536, 256], P(('rows', 'grp')), may hold values from -6 to 6
- label: int32 [65536], P(('rows', 'grp')), may hold values 0 or 1
Outputs:
- pooled: float32 [65536, 256], P(('rows', 'grp'))
- new_table: float32 [524288, 256], P(('rows', 'grp'))
- hot_new: float32 [4096, 256], replicated
Inputs may be any that keep to these rules, and one draw needn't show every extreme that they name: `hot_slot`: distinct within each device's block of 16 entries; hot row h lies in the shard of device h // 16. `cold_row`: a cold slot never names a hot row of its owner. `cold_bag`: a value of 256 or more marks an empty slot.
All inputs are finite; a program needn't handle non-finite values. No bound on the sum of `label` on one device may be relied on, other than what follows from the above.
Results may differ from a plain program's by a relative error of at most 0.0029.
Values may be sent and summed in bfloat16 or wider, within the bound.
A program may use at most 64 MiB of HBM per device.

v0:
```python
import jax
import jax.numpy as jnp
from jax import lax
from jax.sharding import PartitionSpec as P


def split_up(value, dim, peers):
    shape = value.shape
    blocks = value.reshape(*shape[:dim], peers, shape[dim] // peers, *shape[dim + 1 :])
    return jnp.moveaxis(blocks, dim, 0)


def laid_out(blocks, dim):
    blocks = jnp.moveaxis(blocks, 0, dim)
    shape = blocks.shape
    return blocks.reshape(*shape[:dim], shape[dim] * shape[dim + 1], *shape[dim + 2 :])


def exchange_both(value, axis, axes, splits, concats):
    sizes = [lax.axis_size(a) for a in axes]
    blocks = split_up(value, splits[0], sizes[0])
    blocks = jnp.moveaxis(split_up(blocks, splits[1] + 1, sizes[1]), 0, 1)
    inside = blocks.shape[2:]
    blocks = blocks.reshape(-1, *inside)
    blocks = lax.all_to_all(blocks, axis, split_axis=0, concat_axis=0, tiled=True)
    blocks = laid_out(blocks.reshape(*sizes, *inside), concats[0] + 1)
    return laid_out(blocks, concats[1])


def body(table, hot_slot, cold_row, cold_bag, hot_pick, dense, label):
    n_rows = lax.axis_size("rows")
    n_grp = lax.axis_size("grp")
    width = table.shape[1]
    samples = dense.shape[0]
    own_hot = hot_slot.shape[0]
    slots = cold_row.shape[1] * cold_row.shape[2]
    per_peer = cold_row.shape[2]
    rounded = table.astype(jnp.bfloat16)
    hot_full = lax.all_gather(table[hot_slot], ("rows", "grp"), axis=0, tiled=True)
    hot_copy = hot_full.astype(jnp.bfloat16)
    requests = cold_row[0].reshape(n_rows, n_grp, per_peer)
    arrived = exchange_both(requests, ("rows", "grp"), ("rows", "grp"), (0, 1), (0, 1))
    looked = rounded[arrived.reshape(-1)].reshape(n_rows, n_grp, per_peer, width)
    returned = lax.all_to_all(
        lax.all_to_all(looked, "rows", split_axis=0, concat_axis=0, tiled=True),
        "grp",
        split_axis=1,
        concat_axis=1,
        tiled=True,
    )
    flat_rows = returned.reshape(slots, width)
    bags = cold_bag[0].reshape(slots)
    selector = jnp.arange(samples, dtype=jnp.int32)[:, None] == bags[None, :]
    cold_pooled = jnp.dot(
        selector.astype(jnp.bfloat16), flat_rows, preferred_element_type=jnp.float32
    )
    hot_pooled = jnp.sum(hot_copy[hot_pick].astype(jnp.float32), axis=1)
    pooled = cold_pooled + hot_pooled
    score = jnp.sum(pooled * dense, axis=1) / width**0.5
    err = jax.nn.sigmoid(score) - label.astype(jnp.float32)
    grad = err[:, None] * dense
    slot_grad = lax.dot_general(
        selector.astype(jnp.float32),
        grad,
        (((0,), (0,)), ((), ())),
        precision=lax.Precision.HIGHEST,
        preferred_element_type=jnp.float32,
    )
    delivered = exchange_both(
        slot_grad.reshape(n_rows, n_grp, per_peer, width),
        ("rows", "grp"),
        ("rows", "grp"),
        (0, 1),
        (0, 1),
    )
    table_grad = jax.ops.segment_sum(
        delivered.reshape(slots, width), arrived.reshape(slots), num_segments=table.shape[0]
    )
    hot_total = hot_copy.shape[0]
    spread = jnp.repeat(grad, hot_pick.shape[1], axis=0)
    hot_local = jax.ops.segment_sum(spread, hot_pick.reshape(-1), num_segments=hot_total)
    summed = lax.psum(hot_local, ("rows", "grp"))
    start = lax.axis_index(("rows", "grp")) * own_hot
    own_grad = lax.dynamic_slice_in_dim(summed, start, own_hot, 0)
    table_grad = table_grad.at[hot_slot].add(own_grad)
    new_table = table - 0.1 * table_grad
    hot_new = hot_full - 0.1 * summed
    return (pooled, new_table, hot_new)


def solution(mesh):
    placed = (
        P(("rows", "grp"), None),
        P(("rows", "grp")),
        P(("rows", "grp"), None, None),
        P(("rows", "grp"), None, None),
        P(("rows", "grp"), None),
        P(("rows", "grp"), None),
        P(("rows", "grp")),
    )
    return jax.shard_map(
        body,
        mesh=mesh,
        in_specs=placed,
        out_specs=(P(("rows", "grp"), None), P(("rows", "grp"), None), P()),
        check_vma=False,
    )
```

profile of v0, /device:TPU:2, one launch (start us, length us, event | category | flops | bytes accessed | tf_op | source)
XLA Modules:
  0.0 783.1 jit_solution(3402326476514333365)
XLA Ops:
  8.4 2.8 gather_fusion.1
  11.2 1.5 copy.38
  12.7 14.7 %all-to-all-start = ((s32[256,1,1,8]{3,2,1,0:T(1,128)}), s32[256,1,1,8]{3,2,1,0:T(1,128)S(1)}, u32[]{:S(2)}, u32[]{:S(2)}) async-start(s32[256,1,1,8]{3,2,1,0:T(1,128)} %bitcast), calls=%async_computation | async-start | bytes 262144 | tf_op jit(solution)/shard_map/all_to_all | solution.py:25
  27.4 1.7 convert_element_type.14
  29.1 10.6 %all-to-all-done = s32[256,1,1,8]{3,2,1,0:T(1,128)S(1)} async-done(((s32[256,1,1,8]{3,2,1,0:T(1,128)}), s32[256,1,1,8]{3,2,1,0:T(1,128)S(1)}, u32[]{:S(2)}, u32[]{:S(2)}) %all-to-all-start) | async-done | bytes 8224 | tf_op jit(solution)/shard_map/all_to_all | solution.py:25
  39.8 7.5 gather_fusion
  47.3 34.3 %all_to_all.20 = bf16[64,4,8,256]{3,2,1,0:T(8,128)(2,1)S(1)} all-to-all(bf16[64,4,8,256]{3,2,1,0:T(8,128)(2,1)S(1)} %bitcast.38), channel_id=1, replica_groups=mesh['rows'=64,'grp'=4] {'rows'}, dimensions={0} | all-to-all | bytes 2097152 | tf_op jit(solution)/shard_map/all_to_all | solution.py:45
  81.6 1.0 copy.39
  82.6 4.7 all-to-all-start.2
  88.7 12.2 %all-to-all-done.2 = bf16[64,4,8,256]{3,2,0,1:T(8,128)(2,1)S(1)} async-done(((bf16[64,4,8,256]{3,2,0,1:T(8,128)(2,1)}), bf16[64,4,8,256]{3,2,0,1:T(8,128)(2,1)S(1)}, u32[]{:S(2)}, u32[]{:S(2)}) %all-to-all-start.2) | async-done | bytes 1048608 | tf_op jit(solution)/shard_map/all_to_all | solution.py:44
  100.9 1.1 copy.40
  102.0 330.1 %all-gather.3.cloned.1.call-done = f32[4096,256]{1,0:T(8,128)} async-done(((f32[16,256]{1,0:T(8,128)}), f32[4096,256]{1,0:T(8,128)}) %all-gather.3.cloned.1.call-update) | async-done | bytes 4194320 | tf_op jit(solution)/shard_map/all_gather | solution.py:39
  432.1 2.4 convert_element_type.15
  434.5 7.5 gather_fusion.2
  442.9 2.0 multiply_reduce_fusion
  445.0 3.2 fusion.7
  448.2 9.4 %all-to-all-start.3 = ((f32[256,1,1,8,256]{4,3,2,1,0:T(8,128)}), f32[256,1,1,8,256]{4,3,2,1,0:T(8,128)S(1)}, u32[]{:S(2)}, u32[]{:S(2)}) async-start(f32[256,1,1,8,256]{4,3,2,1,0:T(8,128)} %fusion.7), calls=%async_computation.3 | async-start | bytes 4194304 | tf_op jit(solution)/shard_map/all_to_all | solution.py:25
  458.0 13.8 %scatter_custom_fusion.1 = f32[4096,256]{1,0:T(8,128)} fusion(s32[2048]{0:T(1024)S(1)} %reshape.98, f32[]{:T(128)} %constant.15.clone.1, f32[256,256]{1,0:T(8,128)S(1)} %broadcast_multiply_fusion), kind=kCustom, calls=%fused_computation.10 | custom fusion | flops 524288 | bytes 4456452 | tf_op jit(solution)/shard_map/scatter-add | solution.py:81
  472.0 0.8 copy.46
  472.9 277.2 %all-reduce.2.cloned.1.call-done = f32[4096,256]{1,0:T(8,128)} async-done(((f32[4096,256]{1,0:T(8,128)}), f32[4096,256]{1,0:T(8,128)}) %all-reduce.2.cloned.1.call-update) | async-done | bytes 4194320 | tf_op jit(solution)/shard_map/psum | solution.py:82
  750.1 6.0 multiply_subtract_fusion
  756.1 13.0 %scatter_custom_fusion = f32[2048,256]{1,0:T(8,128)} fusion(s32[2048]{0:T(1024)S(1)} %reshape.90, f32[256,1,1,8,256]{4,3,2,1,0:T(8,128)S(1)} %all-to-all-done.3, f32[]{:T(128)} %constant.15.clone.1), kind=kCustom, calls=%fused_computation.7 | custom fusion | flops 524288 | bytes 4194308 | tf_op jit(solution)/shard_map/scatter-add | solution.py:76
  769.2 3.9 scatter_custom_fusion.2
  773.0 3.2 multiply_subtract_fusion.1
  (38 shorter events, 4.3 us)
Async XLA Ops:
  7.2 425.0 %all-gather.3.cloned.1.call-start = ((), (), s32[]{:S(2)}) async-start(), calls=%async_computation.5 | async-start | bytes 4210688 | tf_op jit(solution)/shard_map/all_gather | solution.py:39
  7.9 0.5 copy-start.6
  12.7 27.0 %all-to-all-start = ((s32[256,1,1,8]{3,2,1,0:T(1,128)}), s32[256,1,1,8]{3,2,1,0:T(1,128)S(1)}, u32[]{:S(2)}, u32[]{:S(2)}) async-start(s32[256,1,1,8]{3,2,1,0:T(1,128)} %bitcast), calls=%async_computation | async-start | bytes 262144 | tf_op jit(solution)/shard_map/all_to_all | solution.py:25
  81.6 5.7 copy-start.1
  81.6 6.6 copy-start.2
  81.6 6.8 copy-start.4
  82.6 18.3 %all-to-all-start.2 = ((bf16[64,4,8,256]{3,2,0,1:T(8,128)(2,1)}), bf16[64,4,8,256]{3,2,0,1:T(8,128)(2,1)S(1)}, u32[]{:S(2)}, u32[]{:S(2)}) async-start(bf16[64,4,8,256]{3,2,0,1:T(8,128)(2,1)} %copy.39), calls=%async_computation.2 | async-start | bytes 2097152 | tf_op jit(solution)/shard_map/all_to_all | solution.py:44
  442.0 2.8 copy-start.5
  448.2 9.6 %copy-start.3 = (s32[256,8]{0,1:T(8,128)S(1)}, s32[256,8]{0,1:T(8,128)}, u32[]{:S(2)}) copy-start(s32[256,8]{0,1:T(8,128)} %param.11) | copy-start | bytes 24580
  448.2 308.0 %all-to-all-start.3 = ((f32[256,1,1,8,256]{4,3,2,1,0:T(8,128)}), f32[256,1,1,8,256]{4,3,2,1,0:T(8,128)S(1)}, u32[]{:S(2)}, u32[]{:S(2)}) async-start(f32[256,1,1,8,256]{4,3,2,1,0:T(8,128)} %fusion.7), calls=%async_computation.3 | async-start | bytes 4194304 | tf_op jit(solution)/shard_map/all_to_all | solution.py:25
  457.5 292.6 %all-reduce.2.cloned.1.call-start = ((), (), s32[]{:S(2)}) async-start(), calls=%async_computation.4 | async-start | bytes 8388608 | tf_op jit(solution)/shard_map/psum | solution.py:82
  769.2 3.9 copy-start
Sparse Core Ops, SparseCore 0:
  11.3 420.7 all-gather.2
  472.0 278.0 all-reduce.1
where the time goes:
time: 784 us; the launch traced here: 783 us
  waiting for transfers between devices  630 us (80%)
  other arithmetic  45.5 us (6%)
  blocking collectives  34.3 us (4%)
  starting transfers between devices  29 us (4%)
  local copies, waits for them, and re-layouts  24.8 us (3%)
  between operations  14.2 us (2%)
    all_gather x1, waiting for transfers between devices, body(): lax.all_gather(table[hot_slot], ('rows', 'grp'), axis=0, tiled=True)  330 us
    psum x1, waiting for transfers between devices, body(): summed = lax.psum(hot_local, ('rows', 'grp'))  277 us
    all_to_all x1, blocking collectives, body(): lax.all_to_all(looked, 'rows', split_axis=0, concat_axis=0, tiled=True)  34.3 us
    all_to_all x2, starting transfers between devices, exchange_both(): lax.all_to_all(blocks, axis, split_axis=0, concat_axis=0, tiled=True)  24 us
  transfers between devices with their start and end apart: 5, of which 4 were waited for; matrix products, arithmetic and copies ran while one was open for 5% of the time, Pallas kernels for 0%

commit v1 on v0

--- a/solution.py
+++ b/solution.py
@@ -79,7 +79,9 @@
     hot_total = hot_copy.shape[0]
     spread = jnp.repeat(grad, hot_pick.shape[1], axis=0)
     hot_local = jax.ops.segment_sum(spread, hot_pick.reshape(-1), num_segments=hot_total)
-    summed = lax.psum(hot_local, ("rows", "grp"))
+    summed = hot_local
+    for nth in ("grp", "rows"):
+        summed = lax.psum(summed, nth)
     start = lax.axis_index(("rows", "grp")) * own_hot
     own_grad = lax.dynamic_slice_in_dim(summed, start, own_hot, 0)
     table_grad = table_grad.at[hot_slot].add(own_grad)

time: 784 us -> 1290 us (1.65)
  waiting for transfers between devices: 630 us -> 1130 us
    psum x1 -> x2, waiting for transfers between devices: 277 us -> 722 us  [body(): summed = lax.psum(summed, nth)]
    all_to_all x2, waiting for transfers between devices: 10.6 us -> 69.1 us  [exchange_both(): lax.all_to_all(blocks, axis, split_axis=0, concat_axis=0, tiled=True)]
  transfers between devices with their start and end apart: 5 -> 6, of which waited for: 4 -> 6; matrix products, arithmetic and copies ran while one was open for 5% -> 3% of each run, Pallas kernels for 0% -> 0%
where the time goes in v1:
time: 1290 us
  waiting for transfers between devices  1130 us (88%)
  other arithmetic  44.4 us (3%)
  blocking collectives  34.3 us (3%)
  starting transfers between devices  33.8 us (3%)
  local copies, waits for them, and re-layouts  25.4 us (2%)
  between operations  13.9 us (1%)
    psum x2, waiting for transfers between devices, body(): summed = lax.psum(summed, nth)  722 us
    all_gather x1, waiting for transfers between devices, body(): lax.all_gather(table[hot_slot], ('rows', 'grp'), axis=0, tiled=True)  330 us
    all_to_all x2, waiting for transfers between devices, exchange_both(): lax.all_to_all(blocks, axis, split_axis=0, concat_axis=0, tiled=True)  69.1 us
    all_to_all x1, blocking collectives, body(): lax.all_to_all(looked, 'rows', split_axis=0, concat_axis=0, tiled=True)  34.3 us
    all_to_all x2, starting transfers between devices, exchange_both(): lax.all_to_all(blocks, axis, split_axis=0, concat_axis=0, tiled=True)  29 us
  transfers between devices with their start and end apart: 6, of which 6 were waited for; matrix products, arithmetic and copies ran while one was open for 3% of the time, Pallas kernels for 0%

profile of v1, /device:TPU:2, one launch (start us, length us, event | category | flops | bytes accessed | tf_op | source)
XLA Modules:
  0.0 1289.9 jit_solution(18073150162778733575)
XLA Ops:
  8.5 2.8 gather_fusion.1
  11.2 1.5 copy.38
  12.7 14.7 %all-to-all-start = ((s32[256,1,1,8]{3,2,1,0:T(1,128)}), s32[256,1,1,8]{3,2,1,0:T(1,128)S(1)}, u32[]{:S(2)}, u32[]{:S(2)}) async-start(s32[256,1,1,8]{3,2,1,0:T(1,128)} %bitcast), calls=%async_computation | async-start | bytes 262144 | tf_op jit(solution)/shard_map/all_to_all | solution.py:25
  27.4 1.7 convert_element_type.14
  29.1 10.6 all-to-all-done
  39.9 7.5 gather_fusion
  47.4 34.3 %all_to_all.20 = bf16[64,4,8,256]{3,2,1,0:T(8,128)(2,1)S(1)} all-to-all(bf16[64,4,8,256]{3,2,1,0:T(8,128)(2,1)S(1)} %bitcast.38), channel_id=1, replica_groups=mesh['rows'=64,'grp'=4] {'rows'}, dimensions={0} | all-to-all | bytes 2097152 | tf_op jit(solution)/shard_map/all_to_all | solution.py:45
  82.7 4.7 all-to-all-start.2
  89.6 11.4 all-to-all-done.2
  101.0 1.1 copy.40
  102.1 330.1 %all-gather.3.cloned.1.call-done = f32[4096,256]{1,0:T(8,128)} async-done(((f32[16,256]{1,0:T(8,128)}), f32[4096,256]{1,0:T(8,128)}) %all-gather.3.cloned.1.call-update) | async-done | bytes 4194320 | tf_op jit(solution)/shard_map/all_gather | solution.py:39
  432.2 2.4 convert_element_type.15
  434.6 7.5 gather_fusion.2
  443.0 2.0 multiply_reduce_fusion
  445.1 14.0 %scatter_custom_fusion.1 = f32[4096,256]{1,0:T(8,128)} fusion(s32[2048]{0:T(1024)} %reshape.98, f32[]{:T(128)} %constant.15.clone.1, f32[256,256]{1,0:T(8,128)S(1)} %broadcast_multiply_fusion), kind=kCustom, calls=%fused_computation.10 | custom fusion | flops 524288 | bytes 4456960 | tf_op jit(solution)/shard_map/scatter-add | solution.py:81
  459.1 92.4 %all-reduce.3.cloned.1.call-done = f32[4096,256]{1,0:T(8,128)} async-done(((f32[4096,256]{1,0:T(8,128)}), f32[4096,256]{1,0:T(8,128)}) %all-reduce.3.cloned.1.call-update) | async-done | bytes 4194320 | tf_op jit(solution)/shard_map/psum | solution.py:84
  551.6 3.2 fusion.7
  554.7 14.3 %all-to-all-start.3 = ((f32[256,1,1,8,256]{4,3,2,1,0:T(8,128)}), f32[256,1,1,8,256]{4,3,2,1,0:T(8,128)S(1)}, u32[]{:S(2)}, u32[]{:S(2)}) async-start(f32[256,1,1,8,256]{4,3,2,1,0:T(8,128)} %fusion.7), calls=%async_computation.3 | async-start | bytes 4194304 | tf_op jit(solution)/shard_map/all_to_all | solution.py:25
  570.0 58.5 %all-to-all-done.3 = f32[256,1,1,8,256]{4,3,2,1,0:T(8,128)S(1)} async-done(((f32[256,1,1,8,256]{4,3,2,1,0:T(8,128)}), f32[256,1,1,8,256]{4,3,2,1,0:T(8,128)S(1)}, u32[]{:S(2)}, u32[]{:S(2)}) %all-to-all-start.3) | async-done | bytes 2097184 | tf_op jit(solution)/shard_map/all_to_all | solution.py:25
  628.5 13.0 %scatter_custom_fusion = f32[2048,256]{1,0:T(8,128)} fusion(s32[2048]{0:T(1024)S(1)} %reshape.90, f32[256,1,1,8,256]{4,3,2,1,0:T(8,128)S(1)} %all-to-all-done.3, f32[]{:T(128)} %constant.15.clone.1), kind=kCustom, calls=%fused_computation.7 | custom fusion | flops 524288 | bytes 4194308 | tf_op jit(solution)/shard_map/scatter-add | solution.py:76
  641.5 630.0 %all-reduce.5.cloned.1.call-done = f32[4096,256]{1,0:T(8,128)} async-done(((f32[4096,256]{1,0:T(8,128)}), f32[4096,256]{1,0:T(8,128)}) %all-reduce.5.cloned.1.call-update) | async-done | bytes 4194320 | tf_op jit(solution)/shard_map/psum | solution.py:84
  1271.5 3.7 scatter_custom_fusion.2
  1275.3 3.3 multiply_subtract_fusion.1
  1278.6 4.7 multiply_subtract_fusion
  (41 shorter events, 6.7 us)
Async XLA Ops:
  7.2 425.1 %all-gather.3.cloned.1.call-start = ((), (), s32[]{:S(2)}) async-start(), calls=%async_computation.6 | async-start | bytes 4210688 | tf_op jit(solution)/shard_map/all_gather | solution.py:39
  7.9 0.6 copy-start.6
  12.7 27.0 %all-to-all-start = ((s32[256,1,1,8]{3,2,1,0:T(1,128)}), s32[256,1,1,8]{3,2,1,0:T(1,128)S(1)}, u32[]{:S(2)}, u32[]{:S(2)}) async-start(s32[256,1,1,8]{3,2,1,0:T(1,128)} %bitcast), calls=%async_computation | async-start | bytes 262144 | tf_op jit(solution)/shard_map/all_to_all | solution.py:25
  81.7 5.8 copy-start.2
  81.7 6.6 copy-start.3
  81.7 7.0 copy-start.4
  82.7 18.3 %all-to-all-start.2 = ((bf16[64,4,8,256]{3,2,0,1:T(8,128)(2,1)}), bf16[64,4,8,256]{3,2,0,1:T(8,128)(2,1)S(1)}, u32[]{:S(2)}, u32[]{:S(2)}) async-start(bf16[64,4,8,256]{3,2,0,1:T(8,128)(2,1)} %copy.39), calls=%async_computation.2 | async-start | bytes 2097152 | tf_op jit(solution)/shard_map/all_to_all | solution.py:44
  87.4 464.1 %all-reduce.3.cloned.1.call-start = ((), (), s32[]{:S(2)}) async-start(), calls=%async_computation.4 | async-start | bytes 8388608 | tf_op jit(solution)/shard_map/psum | solution.py:84
  442.1 2.8 copy-start.5
  459.1 812.4 %all-reduce.5.cloned.1.call-start = ((), (), s32[]{:S(2)}) async-start(), calls=%async_computation.5 | async-start | bytes 8388608 | tf_op jit(solution)/shard_map/psum | solution.py:84
  554.7 73.8 %all-to-all-start.3 = ((f32[256,1,1,8,256]{4,3,2,1,0:T(8,128)}), f32[256,1,1,8,256]{4,3,2,1,0:T(8,128)S(1)}, u32[]{:S(2)}, u32[]{:S(2)}) async-start(f32[256,1,1,8,256]{4,3,2,1,0:T(8,128)} %fusion.7), calls=%async_computation.3 | async-start | bytes 4194304 | tf_op jit(solution)/shard_map/all_to_all | solution.py:25
  641.5 633.7 %copy-start.1 = (f32[2048,256]{1,0:T(8,128)S(1)}, f32[2048,256]{1,0:T(8,128)}, u32[]{:S(2)}) copy-start(f32[2048,256]{1,0:T(8,128)} %param.7) | copy-start | bytes 6291460
  1275.3 3.3 copy-start
Sparse Core Ops, SparseCore 0:
  11.4 420.8 all-gather.2
  459.2 92.2 all-reduce.2
  554.2 717.3 all-reduce.4
